TPU v7x, 128 devices: a whole 4x4x4 slice. The times are simulated.
128 devices in a mesh: req: 32 (over x, y, core), mlp: 4 (over z).
Axes of the slice: x: 4, y: 4, z: 4, core: 2. Of those that a mesh axis runs over, the one named last changes fastest.
Arguments:
- hidden_in: bfloat16 [64, 512, 2048], P('req'), may hold values from -6 to 6
- lengths: int32 [64], replicated, may hold values from 1 to 512, 16384 in all
- slot_request: int32 [64], replicated, may hold values from 0 to 63, each once
- adapter_of: int32 [64], replicated, may hold values from 0 to 63, as said below
- adapter_slot: int32 [64], replicated, may hold values from 0 to 63, each once
- norm_gain_attn: float32 [2048], replicated, may hold values from 0.5 to 1.5
- norm_gain_mlp: float32 [2048], replicated, may hold values from 0.5 to 1.5
- final_gain: float32 [2048], replicated, may hold values from 0.5 to 1.5
- w_qkv: bfloat16 [2048, 3, 2048], P(None, None, 'mlp')
- w_out: bfloat16 [2048, 2048], P('mlp'), may hold values from -0.125 to 0.125
- w_gateup: bfloat16 [2048, 2, 4096], P('req', None, 'mlp'), may hold values from -0.125 to 0.125
- w_down: bfloat16 [4096, 2048], P('mlp', 'req'), may hold values from -0.09375 to 0.09375
- adapter_down: bfloat16 [64, 16, 2048], P('req'), may hold values from -0.125 to 0.125
- adapter_up: bfloat16 [64, 16, 2048], P('req', None, 'mlp'), may hold values from -1.5 to 1.5
- vocab: bfloat16 [49152, 2048], P(('req', 'mlp')), may hold values from -0.375 to 0.375
Outputs:
- out_hidden: bfloat16 [64, 512, 2048], P('req')
- request_norm: float32 [64], replicated
- request_peak: float32 [64], replicated
Inputs may be any that keep to these rules, and one draw needn't show every extreme that they name: Some request has exactly 512 tokens, and all lengths together sum to 16384. `slot_request`: each request sits in exactly one slot. `adapter_of`: exactly 16 distinct adapters are named. `adapter_slot`: each adapter sits in exactly one row of the adapter tables.
All inputs are finite; a program needn't handle non-finite values.
Results may differ from a plain program's by a relative error of at most 0.018.
Values may be sent and summed in bfloat16 or wider, within the bound.
A program may use at most 128 MiB of HBM per device.

v0:
```python
import jax
import jax.numpy as jnp
from jax import lax
from jax.sharding import PartitionSpec as P

HEAD_WIDTH = 64
EPSILON = 1e-05
ROPE_BASE = 130000.0
ADAPTER_SCALE = 2.0
MASKED = -1e30


def rms_norm(values, gain):
    return values * lax.rsqrt(jnp.mean(values * values, axis=-1, keepdims=True) + EPSILON) * gain


def rotary_embedded(tensor):
    length = tensor.shape[-3]
    half_width = tensor.shape[-1] // 2
    frequency = ROPE_BASE ** (-(jnp.arange(half_width, dtype=jnp.float32) * 2.0 / tensor.shape[-1]))
    angles = jnp.arange(length, dtype=jnp.float32)[:, None] * frequency[None, :]
    cosine = jnp.cos(angles)[:, None, :]
    sine_part = jnp.sin(angles)[:, None, :]
    front_half = tensor[..., :half_width]
    back_half = tensor[..., half_width:]
    return jnp.concatenate(
        [front_half * cosine - back_half * sine_part, back_half * cosine + front_half * sine_part],
        axis=-1,
    )


def per_device(
    hidden_in,
    lengths,
    slot_request,
    adapter_of,
    adapter_slot,
    norm_gain_attn,
    norm_gain_mlp,
    final_gain,
    w_qkv,
    w_out,
    w_gateup,
    w_down,
    adapter_down,
    adapter_up,
    vocab,
):
    req_index = lax.axis_index("req")
    slots_number, sequence_length, width = hidden_in.shape
    row_count = slots_number * sequence_length
    head_cols = w_qkv.shape[2]
    heads_number = head_cols // HEAD_WIDTH
    unit_cols = w_gateup.shape[2]
    requests = lax.dynamic_slice_in_dim(slot_request, req_index * slots_number, slots_number)
    own_lengths = jnp.take(lengths, requests)
    own_adapters = jnp.take(adapter_of, requests)
    table_rows = jnp.take(adapter_slot, own_adapters)
    positions = jnp.arange(sequence_length, dtype=jnp.int32)
    residual_in = hidden_in.astype(jnp.float32)
    normed = rms_norm(residual_in, norm_gain_attn).astype(jnp.bfloat16)
    projected_rows = jnp.dot(
        normed.reshape(row_count, width),
        w_qkv.reshape(width, 3 * head_cols),
        preferred_element_type=jnp.float32,
    ).reshape(slots_number, sequence_length, 3, head_cols)
    down_all, up_all = (
        lax.all_gather(adapter_down, "req", axis=0, tiled=True),
        lax.all_gather(adapter_up, "req", axis=0, tiled=True),
    )
    down_rows = jnp.take(down_all, table_rows, axis=0)
    up_rows = jnp.take(up_all, table_rows, axis=0)
    low_rank = jnp.einsum(
        "bsd,brd->bsr", normed, down_rows, preferred_element_type=jnp.float32
    ).astype(jnp.bfloat16)
    raised_rows = jnp.einsum("bsr,brc->bsc", low_rank, up_rows, preferred_element_type=jnp.float32)
    queries = rotary_embedded(
        (projected_rows[:, :, 0] + ADAPTER_SCALE * raised_rows).reshape(
            slots_number, sequence_length, heads_number, HEAD_WIDTH
        )
    ).astype(jnp.bfloat16)
    key_heads = rotary_embedded(
        projected_rows[:, :, 1].reshape(slots_number, sequence_length, heads_number, HEAD_WIDTH)
    ).astype(jnp.bfloat16)
    value_heads = (
        projected_rows[:, :, 2]
        .reshape(slots_number, sequence_length, heads_number, HEAD_WIDTH)
        .astype(jnp.bfloat16)
    )
    causal = positions[None, :] <= positions[:, None]

    def attend(slot_items):
        query_one, key_one, value_one, length = slot_items
        scores = jnp.einsum(
            "qhd,khd->hqk", query_one, key_one, preferred_element_type=jnp.float32
        ) * HEAD_WIDTH ** (-0.5)
        allowed = causal & (positions[None, :] < length)
        scores = jnp.where(allowed[None], scores, MASKED)
        probabilities = jax.nn.softmax(scores, axis=-1).astype(jnp.bfloat16)
        return jnp.einsum(
            "hqk,khd->qhd", probabilities, value_one, preferred_element_type=jnp.float32
        ).astype(jnp.bfloat16)

    attended = lax.map(attend, (queries, key_heads, value_heads, own_lengths))
    head_part = jnp.dot(
        attended.reshape(row_count, head_cols), w_out, preferred_element_type=jnp.float32
    )
    mixed_heads = lax.psum(head_part.astype(jnp.bfloat16), "mlp").astype(jnp.float32)
    stream = (residual_in + mixed_heads.reshape(slots_number, sequence_length, width)).astype(
        jnp.bfloat16
    )
    normed_mid = (
        rms_norm(stream.astype(jnp.float32), norm_gain_mlp)
        .astype(jnp.bfloat16)
        .reshape(row_count, width)
    )
    shard_piece = lax.all_gather(w_gateup, "req", axis=0, tiled=True)
    gate_up = jnp.dot(
        normed_mid,
        shard_piece.reshape(shard_piece.shape[0], 2 * unit_cols),
        preferred_element_type=jnp.float32,
    )
    activated = (jax.nn.silu(gate_up[:, :unit_cols]) * gate_up[:, unit_cols:]).astype(jnp.bfloat16)
    unit_part = jnp.dot(
        activated,
        lax.all_gather(w_down, "req", axis=1, tiled=True),
        preferred_element_type=jnp.float32,
    )
    unit_total = lax.psum(unit_part.astype(jnp.bfloat16), "mlp").astype(jnp.float32)
    result = stream.astype(jnp.float32) + unit_total.reshape(slots_number, sequence_length, width)
    live = positions[None, :] < own_lengths[:, None]
    out_hidden = jnp.where(live[:, :, None], result, 0.0).astype(jnp.bfloat16)
    out_float = out_hidden.astype(jnp.float32)
    square_sum = jnp.sum(out_float * out_float, axis=(1, 2))
    slot_norm = jnp.sqrt(square_sum / (own_lengths.astype(jnp.float32) * width))
    picked = (positions[None, :] == own_lengths[:, None] - 1).astype(jnp.float32)
    last_rows = jnp.einsum("bs,bsd->bd", picked, out_float, precision=lax.Precision.HIGHEST)
    last_rounded = lax.optimization_barrier(rms_norm(last_rows, final_gain).astype(jnp.bfloat16))
    last_normed = last_rounded.astype(jnp.float32)
    every_last, every_norm = (
        lax.all_gather(last_normed, "req", axis=0, tiled=True),
        lax.all_gather(slot_norm, "req", axis=0, tiled=True),
    )
    logits = lax.dot_general(
        every_last.astype(jnp.bfloat16),
        vocab,
        (((1,), (1,)), ((), ())),
        preferred_element_type=jnp.float32,
    )
    slot_peak = lax.pmax(jnp.max(logits, axis=1), ("req", "mlp"))
    request_total = slot_request.shape[0]
    owners = slot_request[None, :] == jnp.arange(request_total, dtype=jnp.int32)[:, None]
    request_norm = jnp.sum(jnp.where(owners, every_norm[None, :], 0.0), axis=1)
    request_peak = jnp.sum(jnp.where(owners, slot_peak[None, :], 0.0), axis=1)
    return (out_hidden, request_norm, request_peak)


def solution(mesh):
    return jax.shard_map(
        per_device,
        mesh=mesh,
        in_specs=(
            P("req", None, None),
            P(),
            P(),
            P(),
            P(),
            P(),
            P(),
            P(),
            P(None, None, "mlp"),
            P("mlp", None),
            P("req", None, "mlp"),
            P("mlp", "req"),
            P("req", None, None),
            P("req", None, "mlp"),
            P(("req", "mlp"), None),
        ),
        out_specs=(P("req", None, None), P(), P()),
        check_vma=False,
    )
```

profile of v0, /device:TPU:0, one launch (start us, length us, event | category | flops | bytes accessed | tf_op | source)
XLA Modules:
  0.0 623.8 jit_solution(15625885839021791205)
XLA Ops:
  7.2 0.7 all-gather.8.cloned.1.call-update
  8.0 0.7 all-gather.6.cloned.1.call-update
  8.7 8.8 %copy.26 = bf16[2048,3,512]{0,2,1:T(8,128)(2,1)} copy(bf16[2048,3,512]{2,0,1:T(8,128)(2,1)} %param.27) | data formatting | bytes 12582912 | tf_op args[8]
  17.5 3.2 fusion.44
  21.0 9.1 %fusion.53 = f32[2,512,3,512]{1,3,2,0:T(8,128)S(1)} fusion(bf16[2048,3,512]{0,2,1:T(8,128)(2,1)} %copy.26, bf16[2,512,2048]{2,1,0:T(8,128)(2,1)S(1)} %copy-done.4, f32[2048]{0:T(1024)S(1)} %copy-done.13, f32[2,512]{1,0:T(2,128)S(1)} %add_rsqrt_fusion.1), kind=kOutput, calls=%fused_computation.55 | convolution fusion | flops 6450839552 | bytes 16789504 | tf_op jit(solution)/shard_map/dot_general | solution.py:62
  30.1 1.7 slice.51
  31.8 1.6 copy-done.9
  33.6 0.6 gather_fusion.2
  34.2 0.6 gather_fusion.3
  35.0 0.6 gather_fusion.4
  36.0 19.5 %all-gather.8.cloned.1.call-done = bf16[64,16,512]{2,1,0:T(8,128)(2,1)} async-done(((bf16[2,16,512]{2,1,0:T(8,128)(2,1)}), bf16[64,16,512]{2,1,0:T(8,128)(2,1)}) %all-gather.8.cloned.1.call-update) | async-done | bytes 1048592 | tf_op jit(solution)/shard_map/all_gather | solution.py:69
  55.4 1.8 gather_fusion.1
  57.2 45.8 %all-gather.6.cloned.1.call-done = bf16[64,16,2048]{2,1,0:T(8,128)(2,1)} async-done(((bf16[2,16,2048]{2,1,0:T(8,128)(2,1)}), bf16[64,16,2048]{2,1,0:T(8,128)(2,1)}) %all-gather.6.cloned.1.call-update) | async-done | bytes 4194320 | tf_op jit(solution)/shard_map/all_gather | solution.py:68
  103.0 2.7 gather_fusion
  105.8 5.8 fusion.61
  111.6 2.9 subtract_convert_fusion
  114.4 1.5 pad_maximum_fusion
  116.0 28.0 %while.11 = (s32[]{:T(128)}, bf16[2,512,8,64]{1,3,2,0:T(8,128)(2,1)}, bf16[2,512,8,64]{1,3,2,0:T(8,128)(2,1)S(1)}, s32[2]{0:T(128)S(1)}, bf16[2,512,8,64]{1,3,2,...) while((s32[]{:T(128)}, bf16[2,512,8,64]{1,3,2,0:T(8,128)(2,1)}, ...), condition=%wide.region_4.6_spmd.clone, body=%wide.region_1.5_spmd.clone.sunk | while | flops 550241280 | bytes 19434588 | solution.py:104
  116.0 0.6 dynamic_slice.68
  116.6 0.6 iota_compare_fusion.5
  117.3 7.6 %fusion.116 = (f32[8,512]{1,0:T(8,128)S(1)}, f32[8,512,512]{1,2,0:T(8,128)}) fusion(pred[512,512]{0,1:T(8,128)(4,1)S(1)} %fusion.115, bf16[2,512,8,64]{1,3,2,0:T(8,128)(2,1)} %get-tuple-element.155, s32[]{:T(128)} %get-tuple-element.143, bf16[2,512,8,64]{1,3,2,0:T(8,128)(2,1)} %get-tuple-element.154), kind=kOutput, calls=%fused_computation.116.clone.1 | convolution fusion | flops 276824576 | bytes 9716736 | tf_op jit(solution)/shard_map/while/body/eval_jaxpr/sub | solution.py:99
  124.9 5.0 fusion.117
  130.0 0.6 dynamic_slice.68
  130.5 0.6 iota_compare_fusion.5
  131.3 7.6 %fusion.116 = (f32[8,512]{1,0:T(8,128)S(1)}, f32[8,512,512]{1,2,0:T(8,128)}) fusion(pred[512,512]{0,1:T(8,128)(4,1)S(1)} %fusion.115, bf16[2,512,8,64]{1,3,2,0:T(8,128)(2,1)} %get-tuple-element.155, s32[]{:T(128)} %get-tuple-element.143, bf16[2,512,8,64]{1,3,2,0:T(8,128)(2,1)} %get-tuple-element.154), kind=kOutput, calls=%fused_computation.116.clone.1 | convolution fusion | flops 276824576 | bytes 9716736 | tf_op jit(solution)/shard_map/while/body/eval_jaxpr/sub | solution.py:99
  138.9 5.0 fusion.117
  143.9 2.3 copy.27
  146.5 4.4 convolution_convert_fusion
  152.2 91.4 %all-reduce.4.cloned.1.call-done = bf16[2,512,2048]{2,1,0:T(8,128)(2,1)} async-done(((bf16[2,512,2048]{2,1,0:T(8,128)(2,1)}), bf16[2,512,2048]{2,1,0:T(8,128)(2,1)}) %all-reduce.4.cloned.1.call-update) | async-done | bytes 4194320 | tf_op jit(solution)/shard_map/psum | solution.py:108
  243.6 5.0 fusion.48
  248.7 0.9 copy-done.6
  249.5 3.6 fusion.50
  253.1 45.4 %all-gather.10.cloned.1.call-done = bf16[2048,2,1024]{2,1,0:T(2,128)(2,1)} async-done(((bf16[64,2,1024]{2,1,0:T(2,128)(2,1)}), bf16[2048,2,1024]{2,1,0:T(2,128)(2,1)}) %all-gather.10.cloned.1.call-update) | async-done | bytes 8388624 | tf_op jit(solution)/shard_map/all_gather | solution.py:117
  298.5 10.3 %copy.33 = bf16[256,8,2,1024]{3,1,2,0:T(8,128)(2,1)} copy(bf16[256,8,2,1024]{3,2,1,0:T(2,128)(2,1)} %bitcast.100) | data formatting | bytes 16777216
  308.8 13.3 %fusion.97 = f32[1024,2048]{1,0:T(8,128)} fusion(bf16[1024,2048]{1,0:T(8,128)(2,1)S(1)} %bitcast.102, bf16[2048,2048]{1,0:T(8,128)(2,1)} %bitcast.101), kind=kOutput, calls=%fused_computation.117 | convolution fusion | flops 8589934592 | bytes 20971520 | tf_op jit(solution)/shard_map/dot_general | solution.py:118
  322.0 24.4 %all-gather.12.cloned.1.call-done = bf16[1024,2048]{0,1:T(8,128)(2,1)} async-done(((bf16[1024,64]{0,1:T(8,128)(2,1)}), bf16[1024,2048]{0,1:T(8,128)(2,1)}) %all-gather.12.cloned.1.call-update) | async-done | bytes 4194320 | tf_op jit(solution)/shard_map/all_gather | solution.py:126
  346.4 11.2 %convolution_convert_fusion.1 = bf16[1024,2048]{1,0:T(8,128)(2,1)} fusion(bf16[1024,2048]{0,1:T(8,128)(2,1)} %all-gather.12.cloned.1.call-done, f32[1024,2048]{1,0:T(8,128)} %fusion.97), kind=kOutput, calls=%fused_computation.61 | convolution fusion | flops 4303355904 | bytes 16777216 | tf_op jit(solution)/shard_map/dot_general | solution.py:124
  357.7 0.6 copy-done.14
  358.3 0.6 dynamic-slice
  359.7 90.6 %all-reduce.6.cloned.1.call-done = bf16[2,512,2048]{2,1,0:T(8,128)(2,1)} async-done(((bf16[2,512,2048]{2,1,0:T(8,128)(2,1)}), bf16[2,512,2048]{2,1,0:T(8,128)(2,1)}) %all-reduce.6.cloned.1.call-update) | async-done | bytes 4194320 | tf_op jit(solution)/shard_map/psum | solution.py:129
  450.3 6.9 %multiply_reduce_fusion = (f32[2]{0:T(128)S(1)}, bf16[2,512,2048]{2,1,0:T(8,128)(2,1)S(1)}) fusion(bf16[2,512,2048]{2,1,0:T(8,128)(2,1)} %all-reduce.6.cloned.1.call-done, bf16[2,512,2048]{2,1,0:T(8,128)(2,1)} %all-reduce.4.cloned.1.call-done, bf16[2,512,2048]{2,1,0:T(8,128)(2,1)} %param.19, pred[2,512]{1,0:T(4,128)(4,1)S(1)} %iota_compare_fusion.3), kind=kLoop, calls=%fused_computation.54 | loop fusion | flops 25165822 | bytes 16778248 | tf_op jit(solution)/shard_map/reduce_sum | solution.py:134
  457.3 2.0 copy-done.7
  459.3 0.7 fusion.82
  460.2 24.8 %all-gather = bf16[32,2,2048]{2,1,0:T(2,128)(2,1)S(1)} all-gather(bf16[1,2,2048]{2,1,0:T(2,128)(2,1)S(1)} %bitcast.109), channel_id=1, replica_groups=mesh['req'=32,'mlp'=4] {'req'}, dimensions={0}, use_global_device_ids=true | all-gather | bytes 270336 | tf_op jit(solution)/shard_map/all_gather | solution.py:141
  485.0 2.1 convolution_reduce_fusion
  487.2 64.5 %pmax.7 = f32[64]{0:T(128)S(1)} all-reduce(f32[64]{0:T(128)S(1)} %convolution_reduce_fusion), channel_id=1, replica_groups=mesh['req'=32,'mlp'=4] {'req','mlp'}, use_global_device_ids=true, to_apply=%region_12.14 | all-reduce | flops 64 | bytes 512 | tf_op jit(solution)/shard_map/pmax | solution.py:150
  551.7 64.6 %all-reduce = f32[64]{0:T(128)S(1)} all-reduce(f32[64]{0:T(128)S(1)} %sqrt_dynamic-update-slice_fusion), channel_id=1, replica_groups=mesh['req'=32,'mlp'=4] {'req'}, use_global_device_ids=true, to_apply=%add | all-reduce | flops 64 | bytes 512
  616.3 0.6 select_reduce_fusion
  (59 shorter events, 3.3 us)
Async XLA Ops:
  7.2 139.3 %copy-start = (bf16[512,2048]{1,0:T(8,128)(2,1)S(1)}, bf16[512,2048]{1,0:T(8,128)(2,1)}, u32[]{:S(2)}) copy-start(bf16[512,2048]{1,0:T(8,128)(2,1)} %param.28) | copy-start | bytes 6291460
  7.2 48.2 %all-gather.8.cloned.1.call-start = ((), (), s32[]{:S(2)}) async-start(), calls=%async_computation.1 | async-start | bytes 1081344 | tf_op jit(solution)/shard_map/all_gather | solution.py:69
  7.9 95.1 %all-gather.6.cloned.1.call-start = ((), (), s32[]{:S(2)}) async-start(), calls=%async_computation | async-start | bytes 4325376 | tf_op jit(solution)/shard_map/all_gather | solution.py:68
  8.7 234.9 %all-reduce.4.cloned.1.call-start = ((), (), s32[]{:S(2)}) async-start(), calls=%async_computation.2 | async-start | bytes 8388608 | tf_op jit(solution)/shard_map/psum | solution.py:108
  17.5 3.4 copy-start.4
  17.5 3.4 copy-start.13
  30.1 3.3 copy-start.9
  30.1 3.4 copy-start.12
  30.1 3.5 copy-start.1
  30.1 4.1 copy-start.2
  30.1 4.9 copy-start.3
  150.9 147.5 %all-gather.10.cloned.1.call-start = ((), (), s32[]{:S(2)}) async-start(), calls=%async_computation.3 | async-start | bytes 8650752 | tf_op jit(solution)/shard_map/all_gather | solution.py:117
  151.5 194.9 %all-gather.12.cloned.1.call-start = ((), (), s32[]{:S(2)}) async-start(), calls=%async_computation.4 | async-start | bytes 4325376 | tf_op jit(solution)/shard_map/all_gather | solution.py:126
  152.1 96.5 %copy-start.10 = (f32[2048]{0:T(1024)S(1)}, f32[2048]{0:T(1024)}, u32[]{:S(2)}) copy-start(f32[2048]{0:T(1024)} %param.25) | copy-start | bytes 24580
  152.1 298.2 %all-reduce.6.cloned.1.call-start = ((), (), s32[]{:S(2)}) async-start(), calls=%async_computation.5 | async-start | bytes 8388608 | tf_op jit(solution)/shard_map/psum | solution.py:129
  243.6 5.1 copy-start.5
  243.6 5.9 copy-start.6
  298.5 10.3 %copy-start.8 = (bf16[2,512,2048]{2,1,0:T(8,128)(2,1)S(1)}, bf16[2,512,2048]{2,1,0:T(8,128)(2,1)}, u32[]{:S(2)}) copy-start(bf16[2,512,2048]{2,1,0:T(8,128)(2,1)} %fusion.50) | copy-start | bytes 12582916
  357.6 0.7 copy-start.14
  457.3 2.0 copy-start.7
  457.3 2.8 copy-start.11
Sparse Core Ops, SparseCore 0:
  10.3 45.0 all-gather.7
  57.7 45.2 all-gather.5
  151.1 92.4 all-reduce.3
  246.0 52.4 all-gather.9
  300.8 45.5 all-gather.11
  357.8 92.4 all-reduce.5
where the time goes:
time: 624 us
  waiting for transfers between devices  320 us (51%)
  blocking collectives  154 us (25%)
  matrix products  71.7 us (11%)
  local copies, waits for them, and re-layouts  37.1 us (6%)
  other arithmetic  26.4 us (4%)
  between operations  15 us (2%)
    psum x1, waiting for transfers between devices, per_device(): lax.psum(head_part.astype(jnp.bfloat16), 'mlp').astype(jnp.float32)  91.4 us
    psum x1, waiting for transfers between devices, per_device(): lax.psum(unit_part.astype(jnp.bfloat16), 'mlp').astype(jnp.float32)  90.6 us
    unnamed x1, blocking collectives  64.6 us
    pmax x1, blocking collectives, per_device(): slot_peak = lax.pmax(jnp.max(logits, axis=1), ('req', 'mlp'))  64.5 us
    all_gather x1, waiting for transfers between devices, per_device(): lax.all_gather(adapter_down, 'req', axis=0, tiled=True)  45.8 us
    all_gather x1, waiting for transfers between devices, per_device(): shard_piece = lax.all_gather(w_gateup, 'req', axis=0, tiled=True)  45.4 us
    unnamed x35, local copies, waits for them, and re-layouts  25.3 us
    all_gather x1, blocking collectives, per_device(): lax.all_gather(last_normed, 'req', axis=0, tiled=True)  24.8 us
  transfers between devices with their start and end apart: 6, of which 6 were waited for; matrix products, arithmetic and copies ran while one was open for 10% of the time, Pallas kernels for 0%

commit v1 on v0

--- a/solution.py
+++ b/solution.py
@@ -8,6 +8,11 @@
 ROPE_BASE = 130000.0
 ADAPTER_SCALE = 2.0
 MASKED = -1e30
+
+
+def swapped_in(shard, axis, d):
+    outgoing = jnp.stack([shard] * lax.axis_size(axis))
+    return jnp.concatenate(lax.all_to_all(outgoing, axis, 0, 0), axis=d)
 
 
 def rms_norm(values, gain):
@@ -121,11 +126,7 @@
         preferred_element_type=jnp.float32,
     )
     activated = (jax.nn.silu(gate_up[:, :unit_cols]) * gate_up[:, unit_cols:]).astype(jnp.bfloat16)
-    unit_part = jnp.dot(
-        activated,
-        lax.all_gather(w_down, "req", axis=1, tiled=True),
-        preferred_element_type=jnp.float32,
-    )
+    unit_part = jnp.dot(activated, swapped_in(w_down, "req", 1), preferred_element_type=jnp.float32)
     unit_total = lax.psum(unit_part.astype(jnp.bfloat16), "mlp").astype(jnp.float32)
     result = stream.astype(jnp.float32) + unit_total.reshape(slots_number, sequence_length, width)
     live = positions[None, :] < own_lengths[:, None]

time: 624 us -> 600 us (0.962)
  waiting for transfers between devices: 320 us -> 287 us
    all_gather x1 -> x0, waiting for transfers between devices: 24.4 us -> none  [per_device(): lax.all_gather(w_down, 'req', axis=1, tiled=True)]
    psum x1, waiting for transfers between devices: 91.4 us -> 83.8 us  [per_device(): lax.psum(head_part.astype(jnp.bfloat16), 'mlp').astype(jnp.float32)]
    unnamed x35 -> x37, local copies, waits for them, and re-layouts: 25.3 us -> 25.6 us
  transfers between devices with their start and end apart: 6 -> 6, of which waited for: 6 -> 5; matrix products, arithmetic and copies ran while one was open for 10% -> 10% of each run, Pallas kernels for 0% -> 0%
where the time goes in v1:
time: 600 us; the launch traced here: 599 us
  waiting for transfers between devices  287 us (48%)
  blocking collectives  154 us (26%)
  matrix products  71.5 us (12%)
  local copies, waits for them, and re-layouts  39.9 us (7%)
  other arithmetic  26.4 us (4%)
  between operations  14.7 us (2%)
    psum x1, waiting for transfers between devices, per_device(): lax.psum(unit_part.astype(jnp.bfloat16), 'mlp').astype(jnp.float32)  90.9 us
    psum x1, waiting for transfers between devices, per_device(): lax.psum(head_part.astype(jnp.bfloat16), 'mlp').astype(jnp.float32)  83.8 us
    unnamed x1, blocking collectives  64.6 us
    pmax x1, blocking collectives, per_device(): slot_peak = lax.pmax(jnp.max(logits, axis=1), ('req', 'mlp'))  64.5 us
    all_gather x1, waiting for transfers between devices, per_device(): lax.all_gather(adapter_down, 'req', axis=0, tiled=True)  45.8 us
    all_gather x1, waiting for transfers between devices, per_device(): shard_piece = lax.all_gather(w_gateup, 'req', axis=0, tiled=True)  45.4 us
    unnamed x37, local copies, waits for them, and re-layouts  25.6 us
    all_gather x1, blocking collectives, per_device(): lax.all_gather(last_normed, 'req', axis=0, tiled=True)  24.8 us
  transfers between devices with their start and end apart: 6, of which 5 were waited for; matrix products, arithmetic and copies ran while one was open for 10% of the time, Pallas kernels for 0%

profile of v1, /device:TPU:0, one launch (start us, length us, event | category | flops | bytes accessed | tf_op | source)
XLA Modules:
  0.0 599.1 jit_solution(15618792226613991463)
XLA Ops:
  7.2 0.7 all-gather.7.cloned.1.call-update
  8.0 0.7 all-gather.5.cloned.1.call-update
  8.7 8.8 %copy.27 = bf16[2048,3,512]{0,2,1:T(8,128)(2,1)} copy(bf16[2048,3,512]{2,0,1:T(8,128)(2,1)} %param.27) | data formatting | bytes 12582912 | tf_op args[8]
  17.5 3.2 fusion.44
  21.0 9.1 %fusion.53 = f32[2,512,3,512]{1,3,2,0:T(8,128)S(1)} fusion(bf16[2048,3,512]{0,2,1:T(8,128)(2,1)} %copy.27, bf16[2,512,2048]{2,1,0:T(8,128)(2,1)S(1)} %copy-done.4, f32[2048]{0:T(1024)S(1)} %copy-done.14, f32[2,512]{1,0:T(2,128)S(1)} %add_rsqrt_fusion.1), kind=kOutput, calls=%fused_computation.55 | convolution fusion | flops 6450839552 | bytes 16789504 | tf_op jit(solution)/shard_map/dot_general | solution.py:67
  30.1 1.7 slice.51
  31.8 1.6 copy-done.9
  33.6 0.6 gather_fusion.2
  34.2 0.6 gather_fusion.3
  35.0 0.6 gather_fusion.4
  36.0 19.5 %all-gather.7.cloned.1.call-done = bf16[64,16,512]{2,1,0:T(8,128)(2,1)} async-done(((bf16[2,16,512]{2,1,0:T(8,128)(2,1)}), bf16[64,16,512]{2,1,0:T(8,128)(2,1)}) %all-gather.7.cloned.1.call-update) | async-done | bytes 1048592 | tf_op jit(solution)/shard_map/all_gather | solution.py:74
  55.4 1.8 gather_fusion.1
  57.2 45.8 %all-gather.5.cloned.1.call-done = bf16[64,16,2048]{2,1,0:T(8,128)(2,1)} async-done(((bf16[2,16,2048]{2,1,0:T(8,128)(2,1)}), bf16[64,16,2048]{2,1,0:T(8,128)(2,1)}) %all-gather.5.cloned.1.call-update) | async-done | bytes 4194320 | tf_op jit(solution)/shard_map/all_gather | solution.py:73
  103.0 2.7 gather_fusion
  105.8 5.8 fusion.61
  111.6 2.9 subtract_convert_fusion
  114.4 1.5 pad_maximum_fusion
  116.0 28.0 %while.11 = (s32[]{:T(128)}, bf16[2,512,8,64]{1,3,2,0:T(8,128)(2,1)}, bf16[2,512,8,64]{1,3,2,0:T(8,128)(2,1)S(1)}, s32[2]{0:T(128)S(1)}, bf16[2,512,8,64]{1,3,2,...) while((s32[]{:T(128)}, bf16[2,512,8,64]{1,3,2,0:T(8,128)(2,1)}, ...), condition=%wide.region_4.6_spmd.clone, body=%wide.region_1.5_spmd.clone.sunk | while | flops 550241280 | bytes 19434588 | solution.py:109
  116.0 0.6 dynamic_slice.68
  116.6 0.6 iota_compare_fusion.5
  117.3 7.6 %fusion.116 = (f32[8,512]{1,0:T(8,128)S(1)}, f32[8,512,512]{1,2,0:T(8,128)}) fusion(pred[512,512]{0,1:T(8,128)(4,1)S(1)} %fusion.115, bf16[2,512,8,64]{1,3,2,0:T(8,128)(2,1)} %get-tuple-element.155, s32[]{:T(128)} %get-tuple-element.143, bf16[2,512,8,64]{1,3,2,0:T(8,128)(2,1)} %get-tuple-element.154), kind=kOutput, calls=%fused_computation.116.clone.1 | convolution fusion | flops 276824576 | bytes 9716736 | tf_op jit(solution)/shard_map/while/body/eval_jaxpr/sub | solution.py:104
  124.9 5.0 fusion.117
  130.0 0.6 dynamic_slice.68
  130.5 0.6 iota_compare_fusion.5
  131.3 7.6 %fusion.116 = (f32[8,512]{1,0:T(8,128)S(1)}, f32[8,512,512]{1,2,0:T(8,128)}) fusion(pred[512,512]{0,1:T(8,128)(4,1)S(1)} %fusion.115, bf16[2,512,8,64]{1,3,2,0:T(8,128)(2,1)} %get-tuple-element.155, s32[]{:T(128)} %get-tuple-element.143, bf16[2,512,8,64]{1,3,2,0:T(8,128)(2,1)} %get-tuple-element.154), kind=kOutput, calls=%fused_computation.116.clone.1 | convolution fusion | flops 276824576 | bytes 9716736 | tf_op jit(solution)/shard_map/while/body/eval_jaxpr/sub | solution.py:104
  138.9 5.0 fusion.117
  143.9 2.3 copy.28
  146.5 4.3 convolution_convert_fusion
  151.7 2.5 stack.2
  154.3 5.4 all-to-all-start
  159.7 83.8 %all-reduce.4.cloned.1.call-done = bf16[2,512,2048]{2,1,0:T(8,128)(2,1)} async-done(((bf16[2,512,2048]{2,1,0:T(8,128)(2,1)}), bf16[2,512,2048]{2,1,0:T(8,128)(2,1)}) %all-reduce.4.cloned.1.call-update) | async-done | bytes 4194320 | tf_op jit(solution)/shard_map/psum | solution.py:113
  243.5 5.0 fusion.48
  248.6 0.9 copy-done.6
  249.4 3.6 fusion.50
  253.0 45.4 %all-gather.9.cloned.1.call-done = bf16[2048,2,1024]{2,1,0:T(2,128)(2,1)} async-done(((bf16[64,2,1024]{2,1,0:T(2,128)(2,1)}), bf16[2048,2,1024]{2,1,0:T(2,128)(2,1)}) %all-gather.9.cloned.1.call-update) | async-done | bytes 8388624 | tf_op jit(solution)/shard_map/all_gather | solution.py:122
  298.4 10.3 %copy.34 = bf16[256,8,2,1024]{3,1,2,0:T(8,128)(2,1)} copy(bf16[256,8,2,1024]{3,2,1,0:T(2,128)(2,1)} %bitcast.103) | data formatting | bytes 16777216
  308.7 13.2 %fusion.97 = f32[1024,2048]{1,0:T(8,128)} fusion(bf16[1024,2048]{1,0:T(8,128)(2,1)S(1)} %bitcast.105, bf16[2048,2048]{1,0:T(8,128)(2,1)} %bitcast.104), kind=kOutput, calls=%fused_computation.117 | convolution fusion | flops 8589934592 | bytes 20971520 | tf_op jit(solution)/shard_map/dot_general | solution.py:123
  321.9 11.2 %convolution_convert_fusion.1 = bf16[1024,2048]{1,0:T(8,128)(2,1)} fusion(bf16[1024,2048]{0,1:T(8,128)(2,1)} %bitcast.13, f32[1024,2048]{1,0:T(8,128)} %fusion.97), kind=kOutput, calls=%fused_computation.61 | convolution fusion | flops 4303355904 | bytes 16777216 | tf_op jit(solution)/shard_map/dot_general | solution.py:129
  333.1 0.6 copy-done.15
  335.1 90.9 %all-reduce.6.cloned.1.call-done = bf16[2,512,2048]{2,1,0:T(8,128)(2,1)} async-done(((bf16[2,512,2048]{2,1,0:T(8,128)(2,1)}), bf16[2,512,2048]{2,1,0:T(8,128)(2,1)}) %all-reduce.6.cloned.1.call-update) | async-done | bytes 4194320 | tf_op jit(solution)/shard_map/psum | solution.py:130
  426.0 6.9 %multiply_reduce_fusion = (f32[2]{0:T(128)S(1)}, bf16[2,512,2048]{2,1,0:T(8,128)(2,1)S(1)}) fusion(bf16[2,512,2048]{2,1,0:T(8,128)(2,1)} %all-reduce.6.cloned.1.call-done, bf16[2,512,2048]{2,1,0:T(8,128)(2,1)} %all-reduce.4.cloned.1.call-done, bf16[2,512,2048]{2,1,0:T(8,128)(2,1)} %param.19, pred[2,512]{1,0:T(4,128)(4,1)S(1)} %iota_compare_fusion.3), kind=kLoop, calls=%fused_computation.54 | loop fusion | flops 25165822 | bytes 16778248 | tf_op jit(solution)/shard_map/reduce_sum | solution.py:135
  433.0 2.0 copy-done.7
  435.0 0.7 fusion.82
  435.9 24.8 %all-gather = bf16[32,2,2048]{2,1,0:T(2,128)(2,1)S(1)} all-gather(bf16[1,2,2048]{2,1,0:T(2,128)(2,1)S(1)} %bitcast.112), channel_id=1, replica_groups=mesh['req'=32,'mlp'=4] {'req'}, dimensions={0}, use_global_device_ids=true | all-gather | bytes 270336 | tf_op jit(solution)/shard_map/all_gather | solution.py:142
  460.7 2.1 convolution_reduce_fusion
  462.8 64.5 %pmax.7 = f32[64]{0:T(128)S(1)} all-reduce(f32[64]{0:T(128)S(1)} %convolution_reduce_fusion), channel_id=1, replica_groups=mesh['req'=32,'mlp'=4] {'req','mlp'}, use_global_device_ids=true, to_apply=%region_12.14 | all-reduce | flops 64 | bytes 512 | tf_op jit(solution)/shard_map/pmax | solution.py:151
  527.4 64.6 %all-reduce = f32[64]{0:T(128)S(1)} all-reduce(f32[64]{0:T(128)S(1)} %sqrt_dynamic-update-slice_fusion), channel_id=1, replica_groups=mesh['req'=32,'mlp'=4] {'req'}, use_global_device_ids=true, to_apply=%add | all-reduce | flops 64 | bytes 512
  592.0 0.6 select_reduce_fusion
  (61 shorter events, 3.7 us)
Async XLA Ops:
  7.2 139.3 %copy-start = (bf16[512,2048]{1,0:T(8,128)(2,1)S(1)}, bf16[512,2048]{1,0:T(8,128)(2,1)}, u32[]{:S(2)}) copy-start(bf16[512,2048]{1,0:T(8,128)(2,1)} %param.28) | copy-start | bytes 6291460
  7.2 48.2 %all-gather.7.cloned.1.call-start = ((), (), s32[]{:S(2)}) async-start(), calls=%async_computation.2 | async-start | bytes 1081344 | tf_op jit(solution)/shard_map/all_gather | solution.py:74
  7.9 95.1 %all-gather.5.cloned.1.call-start = ((), (), s32[]{:S(2)}) async-start(), calls=%async_computation.1 | async-start | bytes 4325376 | tf_op jit(solution)/shard_map/all_gather | solution.py:73
  8.7 234.9 %all-reduce.4.cloned.1.call-start = ((), (), s32[]{:S(2)}) async-start(), calls=%async_computation.3 | async-start | bytes 8388608 | tf_op jit(solution)/shard_map/psum | solution.py:113
  17.5 3.4 copy-start.4
  17.5 3.4 copy-start.14
  30.1 3.3 copy-start.9
  30.1 3.4 copy-start.13
  30.1 3.5 copy-start.1
  30.1 4.1 copy-start.2
  30.1 4.9 copy-start.3
  150.8 0.9 copy-start.10
  150.9 147.5 %all-gather.9.cloned.1.call-start = ((), (), s32[]{:S(2)}) async-start(), calls=%async_computation.4 | async-start | bytes 8650752 | tf_op jit(solution)/shard_map/all_gather | solution.py:122
  154.3 167.6 %all-to-all-start = ((bf16[32,1024,64]{1,2,0:T(8,128)(2,1)}), bf16[32,1024,64]{1,2,0:T(8,128)(2,1)}, u32[]{:S(2)}, u32[]{:S(2)}) async-start(bf16[32,1024,64]{1,2,0:T(8,128)(2,1)} %stack.2), calls=%async_computation | async-start | bytes 8388608 | tf_op jit(solution)/shard_map/all_to_all | solution.py:15
  159.7 88.9 %copy-start.11 = (f32[2048]{0:T(1024)S(1)}, f32[2048]{0:T(1024)}, u32[]{:S(2)}) copy-start(f32[2048]{0:T(1024)} %param.25) | copy-start | bytes 24580
  159.7 266.3 %all-reduce.6.cloned.1.call-start = ((), (), s32[]{:S(2)}) async-start(), calls=%async_computation.5 | async-start | bytes 8388608 | tf_op jit(solution)/shard_map/psum | solution.py:130
  243.5 5.1 copy-start.5
  243.5 5.9 copy-start.6
  298.4 10.3 %copy-start.8 = (bf16[2,512,2048]{2,1,0:T(8,128)(2,1)S(1)}, bf16[2,512,2048]{2,1,0:T(8,128)(2,1)}, u32[]{:S(2)}) copy-start(bf16[2,512,2048]{2,1,0:T(8,128)(2,1)} %fusion.50) | copy-start | bytes 12582916
  333.1 0.7 copy-start.15
  432.9 2.0 copy-start.7
  432.9 2.8 copy-start.12
Sparse Core Ops, SparseCore 0:
  10.3 45.0 all-gather.6
  57.7 45.2 all-gather.4
  151.0 92.4 all-reduce.3
  245.9 52.4 all-gather.8
  333.2 92.7 all-reduce.5
